TPU v7x, 128 devices: a whole 4x4x4 slice. The times are simulated.
128 devices in a mesh: replica: 16 (over z_lo, x, core), shard: 8 (over y, z_hi).
Axes of the slice: x: 4, y: 4, z: 4 (z_hi: 2, z_lo: 2; z = z_hi * 2 + z_lo), core: 2. Of those that a mesh axis runs over, the one named last changes fastest.
Arguments:
- params: float32 [16, 128, 28672], P('replica', 'shard'), may hold values from -6 to 6
- first_moment: float32 [16, 128, 28672], P('replica', 'shard'), may hold values from -3 to 3
- second_moment: float32 [16, 128, 28672], P('replica', 'shard'), may hold values from 0.25 to 4
- grads: bfloat16 [4, 16, 128, 28672], P(None, 'replica', 'shard'), may hold values from -6 to 6
- push_weight: float32 [16], P('replica'), may hold values from 0.5 to 2
Outputs:
- final_weights: bfloat16 [16, 128, 28672], P('replica')
All inputs are finite; a program needn't handle non-finite values.
Results may differ from a plain program's by a relative error of at most 0.001.
Values may be sent and summed in bfloat16 or wider, within the bound.
No kernel may reach another device: no remote copies, remote signals or barrier semaphores. Data moves between devices by JAX's collectives and lax.ppermute only.
A program may use at most 64 MiB of HBM per device.

v0:
```python
import jax
import jax.numpy as jnp
from jax import lax
from jax.sharding import PartitionSpec as P

STEPS = 4
beta_one = 0.9
beta_two = 0.95
learn_rate = 0.1
decay_rate = 0.1
epsilon = 1e-08
adam_offset = 101


def passed_along(value, axis, steps):
    count = lax.axis_size(axis)
    pairs = [(source, (source + steps) % count) for source in range(count)]
    return lax.ppermute(value, axis, pairs)


def adam_block(numer, first_moment, second_moment, gradient, weight, first_fix, second_fix):
    scale = weight[:, None, None]
    current = numer / scale
    gradient = gradient.astype(jnp.float32)
    first_moment = beta_one * first_moment + (1.0 - beta_one) * gradient
    second_moment = beta_two * second_moment + (1.0 - beta_two) * gradient * gradient
    update = first_moment / first_fix / (jnp.sqrt(second_moment / second_fix) + epsilon)
    current = current - learn_rate * (update + decay_rate * current)
    return (current * scale, first_moment, second_moment)


def per_device(params, first_moment, second_moment, grads, push_weight):
    replicas = lax.axis_size("replica")
    levels = replicas.bit_length() - 1
    weight = push_weight
    numer = params * weight[:, None, None]
    for iteration in range(STEPS):
        distance = 2 ** (iteration % levels)
        count = adam_offset + iteration
        first_fix = 1.0 - beta_one**count
        second_fix = 1.0 - beta_two**count
        gradient = grads[iteration]
        numer, first_moment, second_moment = adam_block(
            numer, first_moment, second_moment, gradient, weight, first_fix, second_fix
        )
        arrived, arrived_weight = passed_along((numer, weight), "replica", distance)
        numer = 0.5 * numer + 0.5 * arrived
        weight = 0.5 * weight + 0.5 * arrived_weight
    result = (numer / weight[:, None, None]).astype(jnp.bfloat16)
    return lax.all_gather(result, "shard", axis=1, tiled=True)


def solution(mesh):
    return jax.shard_map(
        per_device,
        mesh=mesh,
        in_specs=(
            P("replica", "shard", None),
            P("replica", "shard", None),
            P("replica", "shard", None),
            P(None, "replica", "shard", None),
            P("replica"),
        ),
        out_specs=P("replica", None, None),
        check_vma=False,
    )
```

profile of v0, /device:TPU:1, one launch (start us, length us, event | category | flops | bytes accessed | tf_op | source)
XLA Modules:
  0.0 283.7 jit_solution(8978683002006352249)
XLA Ops:
  6.5 0.0 all-gather.2.cloned.1.call-start
  7.2 0.0 copy-start
  7.2 0.0 copy-start.1
  7.2 0.0 copy-start.2
  7.2 4.6 %subtract_multiply_fusion.2 = f32[1,16,28672]{2,1,0:T(8,128)S(1)} fusion(f32[1,16,28672]{2,1,0:T(8,128)} %param.5, f32[1,16,28672]{2,1,0:T(8,128)} %param.6, f32[1,16,28672]{2,1,0:T(8,128)} %param.7, f32[]{:T(128)} %bitcast.45, bf16[4,1,16,28672]{3,2,1,0:T(8,128)(2,1)} %param.8), kind=kLoop, calls=%fused_computation.32 | loop fusion | flops 8716288 | bytes 8257540 | tf_op jit(solution)/shard_map/mul | solution.py:29
  11.8 2.7 collective-permute-start
  14.5 0.1 collective-permute-start.1
  14.6 20.1 %collective-permute-done.1 = f32[1]{0:T(128)} collective-permute-done((f32[1]{0:T(128)}, f32[1]{0:T(128)}, u32[]{:S(2)}, u32[]{:S(2)}) %collective-permute-start.1) | collective-permute-done | bytes 36 | tf_op jit(solution)/shard_map/ppermute | solution.py:18
  35.2 0.0 collective-permute-done
  35.3 0.0 copy-done
  35.3 0.0 copy-done.1
  35.3 0.0 copy-done.2
  35.3 2.2 subtract_multiply_fusion.1
  37.5 1.3 collective-permute-start.2
  38.8 37.3 %collective-permute-start.3 = (f32[1]{0:T(128)}, f32[1]{0:T(128)}, u32[]{:S(2)}, u32[]{:S(2)}) collective-permute-start(f32[1]{0:T(128)} %add.83), channel_id=1, source_target_pairs={{0,16},{8,24},{16,32},{24,40},{32,48},{40,56},{48,64},{56,72},{64,... | collective-permute-start | bytes 20 | tf_op jit(solution)/shard_map/ppermute | solution.py:18
  76.1 1.6 collective-permute-done.3
  78.2 0.0 collective-permute-done.2
  78.2 2.7 subtract_multiply_fusion
  80.9 2.2 collective-permute-start.4
  83.1 36.5 %collective-permute-start.5 = (f32[1]{0:T(128)}, f32[1]{0:T(128)}, u32[]{:S(2)}, u32[]{:S(2)}) collective-permute-start(f32[1]{0:T(128)} %add.89), channel_id=1, source_target_pairs={{0,32},{8,40},{16,48},{24,56},{32,64},{40,72},{48,80},{56,88},{64,... | collective-permute-start | bytes 20 | tf_op jit(solution)/shard_map/ppermute | solution.py:18
  119.6 0.7 collective-permute-done.5
  120.8 0.0 collective-permute-done.4
  120.8 3.1 %fusion.12 = f32[1,16,28672]{2,1,0:T(8,128)S(1)} fusion(f32[1,16,28672]{2,1,0:T(8,128)S(1)} %subtract_multiply_fusion, f32[1,16,28672]{2,1,0:T(8,128)S(1)} %collective-permute-done.4, bf16[4,1,16,28672]{3,2,1,0:T(8,128)(2,1)S(1)} %copy-done.2, f32[]{:T(128)} %bitcast.9, f32[1,16,28672]{2,1,0:T(8,128)S(1)} %copy-done, f32[1,16,28672]{2,1,0:T(8,128)S(1)} %copy-done.1), kind=kLoop, calls=%fused_computation.24 | loop fusion | flops 20185088 | bytes 12845060 | tf_op jit(solution)/shard_map/mul | solution.py:29
  124.0 1.6 collective-permute-start.6
  125.5 33.5 %collective-permute-start.7 = (f32[1]{0:T(128)}, f32[1]{0:T(128)}, u32[]{:S(2)}, u32[]{:S(2)}) collective-permute-start(f32[1]{0:T(128)} %add.95), channel_id=1, source_target_pairs={{0,64},{8,72},{16,80},{24,88},{32,96},{40,104},{48,112},{56,120},{... | collective-permute-start | bytes 20 | tf_op jit(solution)/shard_map/ppermute | solution.py:18
  159.1 0.8 collective-permute-done.7
  160.4 0.0 collective-permute-done.6
  160.4 1.2 divide_convert_fusion
  161.7 0.0 all-gather.2.cloned.1.call-update
  161.7 108.4 %all-gather.2.cloned.1.call-done = bf16[1,128,28672]{2,1,0:T(8,128)(2,1)} async-done(((bf16[1,16,28672]{2,1,0:T(8,128)(2,1)}), bf16[1,128,28672]{2,1,0:T(8,128)(2,1)}) %all-gather.2.cloned.1.call-update) | async-done | bytes 7340048 | tf_op jit(solution)/shard_map/all_gather | solution.py:50
  270.1 6.8 %copy.8 = bf16[1,128,28672]{2,1,0:T(8,128)(2,1)} copy(bf16[1,128,28672]{2,1,0:T(8,128)(2,1)} %all-gather.2.cloned.1.call-done) | data formatting | bytes 14680064
Async XLA Ops:
  6.5 263.5 %all-gather.2.cloned.1.call-start = ((), (), s32[]{:S(2)}) async-start(), calls=%async_computation | async-start | bytes 8257536 | tf_op jit(solution)/shard_map/all_gather | solution.py:50
  7.2 28.1 %copy-start = (f32[1,16,28672]{2,1,0:T(8,128)S(1)}, f32[1,16,28672]{2,1,0:T(8,128)}, u32[]{:S(2)}) copy-start(f32[1,16,28672]{2,1,0:T(8,128)} %param.6) | copy-start | bytes 5505028
  7.2 28.1 %copy-start.1 = (f32[1,16,28672]{2,1,0:T(8,128)S(1)}, f32[1,16,28672]{2,1,0:T(8,128)}, u32[]{:S(2)}) copy-start(f32[1,16,28672]{2,1,0:T(8,128)} %param.7) | copy-start | bytes 5505028
  7.2 28.1 %copy-start.2 = (bf16[4,1,16,28672]{3,2,1,0:T(8,128)(2,1)S(1)}, bf16[4,1,16,28672]{3,2,1,0:T(8,128)(2,1)}, u32[]{:S(2)}) copy-start(bf16[4,1,16,28672]{3,2,1,0:T(8,128)(2,1)} %param.8) | copy-start | bytes 11010052
  11.8 23.4 %collective-permute-start = (f32[1,16,28672]{2,1,0:T(8,128)S(1)}, f32[1,16,28672]{2,1,0:T(8,128)S(1)}, u32[]{:S(2)}, u32[]{:S(2)}) collective-permute-start(f32[1,16,28672]{2,1,0:T(8,128)S(1)} %subtract_multiply_fusion.2), channel_id=1, source_target_pairs={{0,8},{8,16},{16,24},{24,32},{32,40},{40,48},{48,56},{56,64},{64,7... | collective-permute-start | bytes 5505032 | tf_op jit(solution)/shard_map/ppermute | solution.py:18
  14.5 20.2 %collective-permute-start.1 = (f32[1]{0:T(128)}, f32[1]{0:T(128)}, u32[]{:S(2)}, u32[]{:S(2)}) collective-permute-start(f32[1]{0:T(128)} %param.9), channel_id=1, source_target_pairs={{0,8},{8,16},{16,24},{24,32},{32,40},{40,48},{48,56},{56,64},{64,7... | collective-permute-start | bytes 20 | tf_op jit(solution)/shard_map/ppermute | solution.py:18
  37.5 40.7 %collective-permute-start.2 = (f32[1,16,28672]{2,1,0:T(8,128)S(1)}, f32[1,16,28672]{2,1,0:T(8,128)S(1)}, u32[]{:S(2)}, u32[]{:S(2)}) collective-permute-start(f32[1,16,28672]{2,1,0:T(8,128)S(1)} %subtract_multiply_fusion.1), channel_id=1, source_target_pairs={{0,16},{8,24},{16,32},{24,40},{32,48},{40,56},{48,64},{56,72},{64,... | collective-permute-start | bytes 5505032 | tf_op jit(solution)/shard_map/ppermute | solution.py:18
  38.8 38.9 %collective-permute-start.3 = (f32[1]{0:T(128)}, f32[1]{0:T(128)}, u32[]{:S(2)}, u32[]{:S(2)}) collective-permute-start(f32[1]{0:T(128)} %add.83), channel_id=1, source_target_pairs={{0,16},{8,24},{16,32},{24,40},{32,48},{40,56},{48,64},{56,72},{64,... | collective-permute-start | bytes 20 | tf_op jit(solution)/shard_map/ppermute | solution.py:18
  80.9 39.9 %collective-permute-start.4 = (f32[1,16,28672]{2,1,0:T(8,128)S(1)}, f32[1,16,28672]{2,1,0:T(8,128)S(1)}, u32[]{:S(2)}, u32[]{:S(2)}) collective-permute-start(f32[1,16,28672]{2,1,0:T(8,128)S(1)} %subtract_multiply_fusion), channel_id=1, source_target_pairs={{0,32},{8,40},{16,48},{24,56},{32,64},{40,72},{48,80},{56,88},{64,... | collective-permute-start | bytes 5505032 | tf_op jit(solution)/shard_map/ppermute | solution.py:18
  83.1 37.2 %collective-permute-start.5 = (f32[1]{0:T(128)}, f32[1]{0:T(128)}, u32[]{:S(2)}, u32[]{:S(2)}) collective-permute-start(f32[1]{0:T(128)} %add.89), channel_id=1, source_target_pairs={{0,32},{8,40},{16,48},{24,56},{32,64},{40,72},{48,80},{56,88},{64,... | collective-permute-start | bytes 20 | tf_op jit(solution)/shard_map/ppermute | solution.py:18
  124.0 36.4 %collective-permute-start.6 = (f32[1,16,28672]{2,1,0:T(8,128)S(1)}, f32[1,16,28672]{2,1,0:T(8,128)S(1)}, u32[]{:S(2)}, u32[]{:S(2)}) collective-permute-start(f32[1,16,28672]{2,1,0:T(8,128)S(1)} %fusion.12), channel_id=1, source_target_pairs={{0,64},{8,72},{16,80},{24,88},{32,96},{40,104},{48,112},{56,120},{... | collective-permute-start | bytes 5505032 | tf_op jit(solution)/shard_map/ppermute | solution.py:18
  125.5 34.3 %collective-permute-start.7 = (f32[1]{0:T(128)}, f32[1]{0:T(128)}, u32[]{:S(2)}, u32[]{:S(2)}) collective-permute-start(f32[1]{0:T(128)} %add.95), channel_id=1, source_target_pairs={{0,64},{8,72},{16,80},{24,88},{32,96},{40,104},{48,112},{56,120},{... | collective-permute-start | bytes 20 | tf_op jit(solution)/shard_map/ppermute | solution.py:18
Sparse Core Ops, SparseCore 0:
  161.8 108.2 all-gather.1
where the time goes:
time: 284 us
  waiting for transfers between devices  132 us (46%)
  starting transfers between devices  115 us (40%)
  between operations  16.4 us (6%)
  other arithmetic  13.8 us (5%)
  local copies, waits for them, and re-layouts  6.79 us (2%)
    ppermute x8, starting transfers between devices, passed_along(): return lax.ppermute(value, axis, pairs)  115 us
    all_gather x1, waiting for transfers between devices, per_device(): return lax.all_gather(result, 'shard', axis=1, tiled=True)  108 us
    ppermute x8, waiting for transfers between devices, passed_along(): return lax.ppermute(value, axis, pairs)  23.2 us
    mul x4, other arithmetic, adam_block(): return (current * scale, first_moment, second_moment)  12.6 us
    unnamed x7, local copies, waits for them, and re-layouts  6.79 us
  transfers between devices with their start and end apart: 9, of which 5 were waited for; matrix products, arithmetic and copies ran while one was open for 0% of the time, Pallas kernels for 0%

commit v1 on v0

--- a/solution.py
+++ b/solution.py
@@ -30,6 +30,13 @@
 
 
 def per_device(params, first_moment, second_moment, grads, push_weight):
+
+    def link_indices(shard_in, k_dim):
+        buffers = []
+        for _ in range(lax.axis_size("shard")):
+            buffers.append(shard_in)
+        return jnp.concatenate(lax.all_to_all(jnp.stack(buffers), "shard", 0, 0), k_dim)
+
     replicas = lax.axis_size("replica")
     levels = replicas.bit_length() - 1
     weight = push_weight
@@ -47,7 +54,7 @@
         numer = 0.5 * numer + 0.5 * arrived
         weight = 0.5 * weight + 0.5 * arrived_weight
     result = (numer / weight[:, None, None]).astype(jnp.bfloat16)
-    return lax.all_gather(result, "shard", axis=1, tiled=True)
+    return link_indices(result, 1)
 
 
 def solution(mesh):

time: 284 us -> 253 us (0.89)
  the two profiles are of different devices: /device:TPU:1 before, /device:TPU:6 now
where the time goes in v1:
time: 253 us
  starting transfers between devices  119 us (47%)
  blocking collectives  87.5 us (35%)
  waiting for transfers between devices  27 us (11%)
  other arithmetic  12.9 us (5%)
  local copies, waits for them, and re-layouts  3.76 us (1%)
  between operations  3.35 us (1%)
    ppermute x8, starting transfers between devices, passed_along(): return lax.ppermute(value, axis, pairs)  119 us
    all_to_all x1, blocking collectives, link_indices(): lax.all_to_all(jnp.stack(buffers), 'shard', 0, 0)  87.5 us
    ppermute x8, waiting for transfers between devices, passed_along(): return lax.ppermute(value, axis, pairs)  27 us
    mul x4, other arithmetic, adam_block(): return (current * scale, first_moment, second_moment)  12.6 us
  transfers between devices with their start and end apart: 8, of which 4 were waited for; matrix products, arithmetic and copies ran while one was open for 0% of the time, Pallas kernels for 0%

profile of v1, /device:TPU:6, one launch (start us, length us, event | category | flops | bytes accessed | tf_op | source)
XLA Modules:
  0.0 253.2 jit_solution(15310507040063948955)
XLA Ops:
  0.7 0.0 copy-start
  0.7 0.0 copy-start.1
  0.7 0.0 copy-start.2
  0.7 4.6 %subtract_multiply_fusion.2 = f32[1,16,28672]{2,1,0:T(8,128)S(1)} fusion(f32[1,16,28672]{2,1,0:T(8,128)} %param.5, f32[1,16,28672]{2,1,0:T(8,128)} %param.6, f32[1,16,28672]{2,1,0:T(8,128)} %param.7, f32[]{:T(128)} %bitcast.48, bf16[4,1,16,28672]{3,2,1,0:T(8,128)(2,1)} %param.8), kind=kLoop, calls=%fused_computation.32 | loop fusion | flops 8716288 | bytes 8257540 | tf_op jit(solution)/shard_map/mul | solution.py:29
  5.3 0.1 collective-permute-start
  5.3 1.9 collective-permute-start.1
  7.3 20.9 %collective-permute-done.1 = f32[1]{0:T(128)} collective-permute-done((f32[1]{0:T(128)}, f32[1]{0:T(128)}, u32[]{:S(2)}, u32[]{:S(2)}) %collective-permute-start.1) | collective-permute-done | bytes 36 | tf_op jit(solution)/shard_map/ppermute | solution.py:18
  28.8 0.0 collective-permute-done
  28.8 0.0 copy-done
  28.8 0.0 copy-done.1
  28.8 0.0 copy-done.2
  28.8 2.2 subtract_multiply_fusion.1
  31.1 4.0 %collective-permute-start.2 = (f32[1,16,28672]{2,1,0:T(8,128)S(1)}, f32[1,16,28672]{2,1,0:T(8,128)S(1)}, u32[]{:S(2)}, u32[]{:S(2)}) collective-permute-start(f32[1,16,28672]{2,1,0:T(8,128)S(1)} %subtract_multiply_fusion.1), channel_id=1, source_target_pairs={{0,16},{8,24},{16,32},{24,40},{32,48},{40,56},{48,64},{56,72},{64,... | collective-permute-start | bytes 5505032 | tf_op jit(solution)/shard_map/ppermute | solution.py:18
  35.1 36.4 %collective-permute-start.3 = (f32[1]{0:T(128)}, f32[1]{0:T(128)}, u32[]{:S(2)}, u32[]{:S(2)}) collective-permute-start(f32[1]{0:T(128)} %add.83), channel_id=1, source_target_pairs={{0,16},{8,24},{16,32},{24,40},{32,48},{40,56},{48,64},{56,72},{64,... | collective-permute-start | bytes 20 | tf_op jit(solution)/shard_map/ppermute | solution.py:18
  71.4 1.1 collective-permute-done.3
  73.2 0.0 collective-permute-done.2
  73.2 2.7 %subtract_multiply_fusion = f32[1,16,28672]{2,1,0:T(8,128)S(1)} fusion(f32[1,16,28672]{2,1,0:T(8,128)S(1)} %subtract_multiply_fusion.1, f32[1,16,28672]{2,1,0:T(8,128)S(1)} %collective-permute-done.2, f32[]{:T(128)} %bitcast.6, bf16[4,1,16,28672]{3,2,1,0:T(8,128)(2,1)S(1)} %copy-done.2, f32[1,16,28672]{2,1,0:T(8,128)S(1)} %copy-done, ...), kind=kLoop, calls=%fused_computation.30 | loop fusion | flops 16515072 | bytes 11927556 | tf_op jit(solution)/shard_map/mul | solution.py:29
  75.9 2.5 collective-permute-start.4
  78.4 36.8 %collective-permute-start.5 = (f32[1]{0:T(128)}, f32[1]{0:T(128)}, u32[]{:S(2)}, u32[]{:S(2)}) collective-permute-start(f32[1]{0:T(128)} %add.89), channel_id=1, source_target_pairs={{0,32},{8,40},{16,48},{24,56},{32,64},{40,72},{48,80},{56,88},{64,... | collective-permute-start | bytes 20 | tf_op jit(solution)/shard_map/ppermute | solution.py:18
  115.1 2.7 %collective-permute-done.5 = f32[1]{0:T(128)} collective-permute-done((f32[1]{0:T(128)}, f32[1]{0:T(128)}, u32[]{:S(2)}, u32[]{:S(2)}) %collective-permute-start.5) | collective-permute-done | bytes 36 | tf_op jit(solution)/shard_map/ppermute | solution.py:18
  118.4 0.0 collective-permute-done.4
  118.4 3.1 %fusion.12 = f32[1,16,28672]{2,1,0:T(8,128)S(1)} fusion(f32[1,16,28672]{2,1,0:T(8,128)S(1)} %subtract_multiply_fusion, f32[1,16,28672]{2,1,0:T(8,128)S(1)} %collective-permute-done.4, bf16[4,1,16,28672]{3,2,1,0:T(8,128)(2,1)S(1)} %copy-done.2, f32[]{:T(128)} %bitcast.9, f32[1,16,28672]{2,1,0:T(8,128)S(1)} %copy-done, f32[1,16,28672]{2,1,0:T(8,128)S(1)} %copy-done.1), kind=kLoop, calls=%fused_computation.24 | loop fusion | flops 20185088 | bytes 12845060 | tf_op jit(solution)/shard_map/mul | solution.py:29
  121.6 0.1 collective-permute-start.6
  121.7 36.9 %collective-permute-start.7 = (f32[1]{0:T(128)}, f32[1]{0:T(128)}, u32[]{:S(2)}, u32[]{:S(2)}) collective-permute-start(f32[1]{0:T(128)} %add.95), channel_id=1, source_target_pairs={{0,64},{8,72},{16,80},{24,88},{32,96},{40,104},{48,112},{56,120},{... | collective-permute-start | bytes 20 | tf_op jit(solution)/shard_map/ppermute | solution.py:18
  158.6 2.3 collective-permute-done.7
  161.5 0.0 collective-permute-done.6
  161.6 0.3 fusion.17
  161.9 0.7 stack.2
  162.6 87.5 %all_to_all.5 = bf16[8,1,16,28672]{3,2,1,0:T(8,128)(2,1)S(1)} all-to-all(bf16[8,1,16,28672]{3,2,1,0:T(8,128)(2,1)S(1)} %stack.2), channel_id=1, replica_groups=mesh['replica'=16,'shard'=8] {'shard'}, dimensions={0} | all-to-all | bytes 14680064 | tf_op jit(solution)/shard_map/all_to_all | solution.py:38
  250.1 3.0 %copy.8 = bf16[1,128,28672]{2,1,0:T(8,128)(2,1)} copy(bf16[1,128,28672]{2,1,0:T(8,128)(2,1)S(1)} %bitcast.49) | data formatting | bytes 14680064
Async XLA Ops:
  0.7 28.2 %copy-start = (f32[1,16,28672]{2,1,0:T(8,128)S(1)}, f32[1,16,28672]{2,1,0:T(8,128)}, u32[]{:S(2)}) copy-start(f32[1,16,28672]{2,1,0:T(8,128)} %param.6) | copy-start | bytes 5505028
  0.7 28.2 %copy-start.1 = (f32[1,16,28672]{2,1,0:T(8,128)S(1)}, f32[1,16,28672]{2,1,0:T(8,128)}, u32[]{:S(2)}) copy-start(f32[1,16,28672]{2,1,0:T(8,128)} %param.7) | copy-start | bytes 5505028
  0.7 28.2 %copy-start.2 = (bf16[4,1,16,28672]{3,2,1,0:T(8,128)(2,1)S(1)}, bf16[4,1,16,28672]{3,2,1,0:T(8,128)(2,1)}, u32[]{:S(2)}) copy-start(bf16[4,1,16,28672]{3,2,1,0:T(8,128)(2,1)} %param.8) | copy-start | bytes 11010052
  5.3 23.5 %collective-permute-start = (f32[1,16,28672]{2,1,0:T(8,128)S(1)}, f32[1,16,28672]{2,1,0:T(8,128)S(1)}, u32[]{:S(2)}, u32[]{:S(2)}) collective-permute-start(f32[1,16,28672]{2,1,0:T(8,128)S(1)} %subtract_multiply_fusion.2), channel_id=1, source_target_pairs={{0,8},{8,16},{16,24},{24,32},{32,40},{40,48},{48,56},{56,64},{64,7... | collective-permute-start | bytes 5505032 | tf_op jit(solution)/shard_map/ppermute | solution.py:18
  5.3 22.8 %collective-permute-start.1 = (f32[1]{0:T(128)}, f32[1]{0:T(128)}, u32[]{:S(2)}, u32[]{:S(2)}) collective-permute-start(f32[1]{0:T(128)} %param.9), channel_id=1, source_target_pairs={{0,8},{8,16},{16,24},{24,32},{32,40},{40,48},{48,56},{56,64},{64,7... | collective-permute-start | bytes 20 | tf_op jit(solution)/shard_map/ppermute | solution.py:18
  31.1 42.1 %collective-permute-start.2 = (f32[1,16,28672]{2,1,0:T(8,128)S(1)}, f32[1,16,28672]{2,1,0:T(8,128)S(1)}, u32[]{:S(2)}, u32[]{:S(2)}) collective-permute-start(f32[1,16,28672]{2,1,0:T(8,128)S(1)} %subtract_multiply_fusion.1), channel_id=1, source_target_pairs={{0,16},{8,24},{16,32},{24,40},{32,48},{40,56},{48,64},{56,72},{64,... | collective-permute-start | bytes 5505032 | tf_op jit(solution)/shard_map/ppermute | solution.py:18
  35.1 37.5 %collective-permute-start.3 = (f32[1]{0:T(128)}, f32[1]{0:T(128)}, u32[]{:S(2)}, u32[]{:S(2)}) collective-permute-start(f32[1]{0:T(128)} %add.83), channel_id=1, source_target_pairs={{0,16},{8,24},{16,32},{24,40},{32,48},{40,56},{48,64},{56,72},{64,... | collective-permute-start | bytes 20 | tf_op jit(solution)/shard_map/ppermute | solution.py:18
  75.9 42.5 %collective-permute-start.4 = (f32[1,16,28672]{2,1,0:T(8,128)S(1)}, f32[1,16,28672]{2,1,0:T(8,128)S(1)}, u32[]{:S(2)}, u32[]{:S(2)}) collective-permute-start(f32[1,16,28672]{2,1,0:T(8,128)S(1)} %subtract_multiply_fusion), channel_id=1, source_target_pairs={{0,32},{8,40},{16,48},{24,56},{32,64},{40,72},{48,80},{56,88},{64,... | collective-permute-start | bytes 5505032 | tf_op jit(solution)/shard_map/ppermute | solution.py:18
  78.4 39.4 %collective-permute-start.5 = (f32[1]{0:T(128)}, f32[1]{0:T(128)}, u32[]{:S(2)}, u32[]{:S(2)}) collective-permute-start(f32[1]{0:T(128)} %add.89), channel_id=1, source_target_pairs={{0,32},{8,40},{16,48},{24,56},{32,64},{40,72},{48,80},{56,88},{64,... | collective-permute-start | bytes 20 | tf_op jit(solution)/shard_map/ppermute | solution.py:18
  121.6 40.0 %collective-permute-start.6 = (f32[1,16,28672]{2,1,0:T(8,128)S(1)}, f32[1,16,28672]{2,1,0:T(8,128)S(1)}, u32[]{:S(2)}, u32[]{:S(2)}) collective-permute-start(f32[1,16,28672]{2,1,0:T(8,128)S(1)} %fusion.12), channel_id=1, source_target_pairs={{0,64},{8,72},{16,80},{24,88},{32,96},{40,104},{48,112},{56,120},{... | collective-permute-start | bytes 5505032 | tf_op jit(solution)/shard_map/ppermute | solution.py:18
  121.7 39.2 %collective-permute-start.7 = (f32[1]{0:T(128)}, f32[1]{0:T(128)}, u32[]{:S(2)}, u32[]{:S(2)}) collective-permute-start(f32[1]{0:T(128)} %add.95), channel_id=1, source_target_pairs={{0,64},{8,72},{16,80},{24,88},{32,96},{40,104},{48,112},{56,120},{... | collective-permute-start | bytes 20 | tf_op jit(solution)/shard_map/ppermute | solution.py:18
